TPU v7x, 512 devices: a whole 4x8x8 slice. The times are simulated.
512 devices in a mesh: row: 32 (over y, x_hi, core), col: 16 (over x_lo, z).
Axes of the slice: x: 4 (x_hi: 2, x_lo: 2; x = x_hi * 2 + x_lo), y: 8, z: 8, core: 2. Of those that a mesh axis runs over, the one named last changes fastest.
Arguments:
- perturbation: bfloat16 [16384, 16384], P('row', 'col'), may hold values from -0.046875 to 0.046875
- basis: bfloat16 [16384, 16384], P('row', 'col'), may hold values from -0.125 to 0.125
- orbitals: bfloat16 [16384, 512], P('col', 'row'), may hold values from -6 to 6
- pair_mask: int32 [16384, 512], P('col'), may hold values 0 or 1
- energies: float32 [16384], P('col'), may hold values from 1 to 4
- occ_energies: float32 [512], replicated, may hold values from -3 to -1
Outputs:
- response: float32 [16384, 512], P('row', 'col')
All inputs are finite; a program needn't handle non-finite values. No bound on the sum of `pair_mask` on one device may be relied on, other than what follows from the above.
Results may differ from a plain program's by a relative error of at most 0.0037.
Values may be sent and summed in bfloat16 or wider, within the bound.
No kernel may reach another device: no remote copies, remote signals or barrier semaphores. Data moves between devices by JAX's collectives and lax.ppermute only.
A program may use at most 64 MiB of HBM per device.

v0:
```python
import jax
import jax.numpy as jnp
from jax import lax
from jax.sharding import PartitionSpec as P


def scaled(projection, mask_block, level_block, occ_block):
    spacing = level_block[:, None] - occ_block[None, :]
    return jnp.where(mask_block == 1, projection / spacing, jnp.zeros_like(projection)).astype(
        jnp.bfloat16
    )


def shards(perturbation, basis, orbitals, pair_mask, energies, occ_energies):
    partial_value = jnp.dot(
        perturbation,
        lax.all_gather(orbitals, "row", axis=1, tiled=True),
        preferred_element_type=jnp.float32,
    )
    image = lax.psum(partial_value, "col").astype(jnp.bfloat16)
    row_count = lax.axis_size("row")
    width = pair_mask.shape[1] // row_count
    first = lax.axis_index("row") * width
    project_part = jnp.dot(basis.T, image, preferred_element_type=jnp.float32)
    proj_share = lax.psum_scatter(project_part, "row", scatter_dimension=1, tiled=True)
    mask_block = lax.dynamic_slice_in_dim(pair_mask, first, width, 1)
    occ_block = lax.dynamic_slice_in_dim(occ_energies, first, width, 0)
    coef_share = scaled(proj_share, mask_block, energies, occ_block)
    rotated = jnp.dot(
        basis,
        lax.all_gather(coef_share, "row", axis=1, tiled=True),
        preferred_element_type=jnp.float32,
    )
    return lax.psum_scatter(rotated, "col", scatter_dimension=1, tiled=True)


def solution(mesh):
    return jax.shard_map(
        shards,
        mesh=mesh,
        in_specs=(P("row", "col"), P("row", "col"), P("col", "row"), P("col", None), P("col"), P()),
        out_specs=P("row", "col"),
        check_vma=False,
    )
```

profile of v0, /device:TPU:8, one launch (start us, length us, event | category | flops | bytes accessed | tf_op | source)
XLA Modules:
  0.0 469.6 jit_solution(10693680148405827266)
XLA Ops:
  6.5 0.0 copy-start
  6.5 0.0 all-gather.3.cloned.1.call-start
  6.5 0.7 all-gather.3.cloned.1.call-update
  7.3 0.0 reduce-scatter.7.cloned.1.call-start
  7.3 90.2 %all-gather.3.cloned.1.call-done = bf16[1024,512]{0,1:T(8,128)(2,1)} async-done(((bf16[1024,16]{0,1:T(8,128)(2,1)}), bf16[1024,512]{0,1:T(8,128)(2,1)}) %all-gather.3.cloned.1.call-update) | async-done | bytes 1048592 | tf_op jit(solution)/shard_map/all_gather | solution.py:17
  97.5 2.3 fusion.1
  99.8 77.1 %all-reduce.1 = bf16[512,512]{1,0:T(8,128)(2,1)} all-reduce(f32[512,512]{1,0:T(8,128)S(1)} %fusion.1), channel_id=1, replica_groups=mesh['row'=32,'col'=16] {'col'}, use_global_device_ids=true, to_apply=%region_0.0 | all-reduce | flops 262144 | bytes 1572864 | tf_op jit(solution)/shard_map/psum | solution.py:20
  176.9 0.0 copy-done
  176.9 1.8 convolution_bitcast_fusion
  178.7 1.9 copy.8
  180.6 0.0 copy-start.1
  180.6 0.0 reduce-scatter.7.cloned.1.call-update
  180.6 0.0 all-gather.5.cloned.1.call-start
  180.7 0.8 dynamic_slice.7
  181.4 119.5 %reduce-scatter.7.cloned.1.call-done = f32[16,1024]{1,0:T(8,128)} async-done(((f32[512,1024]{1,0:T(8,128)}), f32[16,1024]{1,0:T(8,128)}) %reduce-scatter.7.cloned.1.call-update) | async-done | bytes 65552
  301.0 1.0 copy.9
  302.0 0.0 copy-done.1
  302.0 1.4 divide_select_fusion
  303.4 0.7 copy.7
  304.1 0.0 all-gather.5.cloned.1.call-update
  304.2 0.0 reduce-scatter.5.cloned.1.call-start
  304.2 81.7 %all-gather.5.cloned.1.call-done = bf16[1024,512]{0,1:T(8,128)(2,1)} async-done(((bf16[1024,16]{0,1:T(8,128)(2,1)}), bf16[1024,512]{0,1:T(8,128)(2,1)}) %all-gather.5.cloned.1.call-update) | async-done | bytes 1048592 | tf_op jit(solution)/shard_map/all_gather | solution.py:31
  385.9 3.0 convolution_bitcast_fusion.1
  388.9 0.0 reduce-scatter.5.cloned.1.call-update
  388.9 74.2 %reduce-scatter.5.cloned.1.call-done = f32[512,32]{0,1:T(8,128)} async-done(((f32[512,512]{0,1:T(8,128)}), f32[512,32]{0,1:T(8,128)}) %reduce-scatter.5.cloned.1.call-update) | async-done | bytes 65552 | tf_op jit(solution)/shard_map/reduce_scatter | solution.py:34
Async XLA Ops:
  6.5 170.4 %copy-start = (bf16[512,1024]{1,0:T(8,128)(2,1)S(1)}, bf16[512,1024]{1,0:T(8,128)(2,1)}, u32[]{:S(2)}) copy-start(bf16[512,1024]{1,0:T(8,128)(2,1)} %param.7) | copy-start | bytes 3145732
  6.5 90.9 %all-gather.3.cloned.1.call-start = ((), (), s32[]{:S(2)}) async-start(), calls=%async_computation.2 | async-start | bytes 1081344 | tf_op jit(solution)/shard_map/all_gather | solution.py:17
  7.3 293.7 %reduce-scatter.7.cloned.1.call-start = ((), (), s32[]{:S(2)}) async-start(), calls=%async_computation.5 | async-start | bytes 2162688
  180.6 121.4 %copy-start.1 = (f32[1024]{0:T(1024)S(1)}, f32[1024]{0:T(1024)}, u32[]{:S(2)}) copy-start(f32[1024]{0:T(1024)} %param.10) | copy-start | bytes 12292
  180.6 205.3 %all-gather.5.cloned.1.call-start = ((), (), s32[]{:S(2)}) async-start(), calls=%async_computation.3 | async-start | bytes 1081344 | tf_op jit(solution)/shard_map/all_gather | solution.py:31
  304.2 158.9 %reduce-scatter.5.cloned.1.call-start = ((), (), s32[]{:S(2)}) async-start(), calls=%async_computation.4 | async-start | bytes 1114112 | tf_op jit(solution)/shard_map/reduce_scatter | solution.py:34
Sparse Core Ops, SparseCore 0:
  10.7 86.7 all-gather.2
  180.7 120.1 reduce-scatter.6
  304.3 81.5 all-gather.4
  389.0 73.9 reduce-scatter.4
where the time goes:
time: 470 us
  waiting for transfers between devices  366 us (78%)
  blocking collectives  77.1 us (16%)
  between operations  13.2 us (3%)
  matrix products  7.1 us (2%)
    unnamed x5, waiting for transfers between devices  120 us
    all_gather x1, waiting for transfers between devices, shards(): lax.all_gather(orbitals, 'row', axis=1, tiled=True)  90.2 us
    all_gather x1, waiting for transfers between devices, shards(): lax.all_gather(coef_share, 'row', axis=1, tiled=True)  81.7 us
    psum x1, blocking collectives, shards(): image = lax.psum(partial_value, 'col').astype(jnp.bfloat16)  77.1 us
    reduce_scatter x1, waiting for transfers between devices, shards(): return lax.psum_scatter(rotated, 'col', scatter_dimension=1, tiled=True)  74.2 us
  transfers between devices with their start and end apart: 4, of which 4 were waited for; matrix products, arithmetic and copies ran while one was open for 0% of the time, Pallas kernels for 0%

commit v1 on v0

v1 whole, which is shorter than its diff:
```python
import jax
import jax.numpy as jnp
from jax import lax
from jax.sharding import Mesh, PartitionSpec as P

ROW = ("y", "xh")
COL = ("xl", "z")
BF16, F32 = jnp.bfloat16, jnp.float32


def exchange(pieces, axes):
    return lax.all_to_all(pieces, axes, 0, 0)


def spread(piece, axes):
    count = lax.axis_size(axes)
    got = exchange(jnp.broadcast_to(piece[None], (count,) + piece.shape), axes)
    return got.reshape((count * piece.shape[0],) + piece.shape[1:])


def collect(part, axes, dtype):
    count = lax.axis_size(axes)
    pieces = part.astype(dtype).reshape((count, part.shape[0] // count) + part.shape[1:])
    return exchange(pieces, axes).astype(F32).sum(axis=0)


def dot_nt(a, b):
    return lax.dot_general(a, b, (((1,), (1,)), ((), ())), preferred_element_type=F32)


def dot_nn(a, b):
    return lax.dot_general(a, b, (((1,), (0,)), ((), ())), preferred_element_type=F32)


def shards(perturbation, basis, orbitals, pair_mask, energies, occ_energies):
    swap = [(0, 1), (1, 0)]
    core = lax.axis_index("core")
    width = orbitals.shape[1]
    rows = perturbation.shape[0]
    pert_other = lax.ppermute(perturbation, "core", swap)
    basis_other = lax.ppermute(basis, "core", swap)

    first = lax.axis_index(ROW + ("core",)) * width
    mask_t = lax.dynamic_slice_in_dim(pair_mask, first, width, 1).T
    occ = lax.dynamic_slice_in_dim(occ_energies, first, width, 0)
    weight = jnp.where(mask_t == 1, 1.0 / (energies[None, :] - occ[:, None]), 0.0)

    orbs = spread(orbitals.T, ROW)
    part = jnp.concatenate([dot_nt(orbs, perturbation), dot_nt(orbs, pert_other)], axis=1)
    image = spread(collect(part, COL, F32).astype(BF16), COL)
    part = dot_nn(image[:, :rows], basis) + dot_nn(image[:, rows:], basis_other)
    coef = spread((collect(part, ROW, BF16) * weight).astype(BF16), ROW)
    part = jnp.concatenate([dot_nt(coef, basis), dot_nt(coef, basis_other)], axis=1)
    mine = collect(part, COL, BF16)
    keep, give = mine[:, :rows], mine[:, rows:]
    got = lax.ppermute(give, "core", swap)
    out = jnp.concatenate(
        [jnp.where(core == 0, keep, got), jnp.where(core == 0, got, keep)], axis=0
    )
    return out.T


def solution(mesh):
    sizes = (mesh.shape["row"] // 4, 2, 2, 2, mesh.shape["col"] // 2)
    fine = Mesh(mesh.devices.reshape(sizes), ("y", "xh", "core", "xl", "z"))
    row, col = ("y", "xh", "core"), ("xl", "z")
    return jax.shard_map(
        shards,
        mesh=fine,
        in_specs=(P(row, col), P(row, col), P(col, row), P(col, None), P(col), P()),
        out_specs=P(row, col),
        check_vma=False,
    )
```

time: 470 us -> 168 us (0.36)
  the two profiles are of different devices: /device:TPU:8 before, /device:TPU:1 now
where the time goes in v1:
time: 168 us; the launch traced here: 167 us
  blocking collectives  76.5 us (46%)
  starting transfers between devices  36 us (21%)
  waiting for transfers between devices  35.7 us (21%)
  matrix products  9.52 us (6%)
  local copies, waits for them, and re-layouts  5.68 us (3%)
  other arithmetic  3.36 us (2%)
    all_to_all x3, blocking collectives, exchange(): return lax.all_to_all(pieces, axes, 0, 0)  76.5 us
    all_to_all x3, waiting for transfers between devices, exchange(): return lax.all_to_all(pieces, axes, 0, 0)  34.9 us
    all_to_all x3, starting transfers between devices, exchange(): return lax.all_to_all(pieces, axes, 0, 0)  23.6 us
    dot_general x4, matrix products, dot_nt(): lax.dot_general(a, b, (((1,), (1,)), ((), ())), preferred_element_type=F32)  5.57 us
    ppermute x1, starting transfers between devices, shards(): got = lax.ppermute(give, 'core', swap)  5.52 us
    ppermute x1, starting transfers between devices, shards(): basis_other = lax.ppermute(basis, 'core', swap)  4.04 us
    dot_general x2, matrix products, dot_nn(): lax.dot_general(a, b, (((1,), (0,)), ((), ())), preferred_element_type=F32)  3.95 us
  transfers between devices with their start and end apart: 6, of which 4 were waited for; matrix products, arithmetic and copies ran while one was open for 4% of the time, Pallas kernels for 0%

profile of v1, /device:TPU:1, one launch (start us, length us, event | category | flops | bytes accessed | tf_op | source)
XLA Modules:
  0.0 167.0 jit_solution(11853180978406311875)
XLA Ops:
  0.0 0.0 copy-start
  0.0 1.8 %broadcast_in_dim.10 = bf16[16,16,1024]{2,1,0:T(8,128)(2,1)} broadcast(bf16[16,1024]{1,0:T(8,128)(2,1)} %bitcast.27), dimensions={1,2} | broadcast | bytes 557056 | tf_op jit(solution)/shard_map/broadcast_in_dim | solution.py:17
  1.8 10.2 %all-to-all-start = ((bf16[16,16,1024]{2,1,0:T(8,128)(2,1)}), bf16[16,16,1024]{2,1,0:T(8,128)(2,1)S(1)}, u32[]{:S(2)}, u32[]{:S(2)}) async-start(bf16[16,16,1024]{2,1,0:T(8,128)(2,1)} %broadcast_in_dim.10), calls=%async_computation | async-start | bytes 1048576 | tf_op jit(solution)/shard_map/all_to_all | solution.py:12
  12.0 2.9 %collective-permute-start = (bf16[512,1024]{1,0:T(8,128)(2,1)}, bf16[512,1024]{1,0:T(8,128)(2,1)}, u32[]{:S(2)}, u32[]{:S(2)}) collective-permute-start(bf16[512,1024]{1,0:T(8,128)(2,1)} %param.6), channel_id=1, source_target_pairs={{0,16},{16,0},{1,17},{17,1},{2,18},{18,2},{3,19},{19,3},{4,20},{20... | collective-permute-start | bytes 3145736 | tf_op jit(solution)/shard_map/ppermute | solution.py:40
  14.9 14.3 %all-to-all-done = bf16[16,16,1024]{2,1,0:T(8,128)(2,1)S(1)} async-done(((bf16[16,16,1024]{2,1,0:T(8,128)(2,1)}), bf16[16,16,1024]{2,1,0:T(8,128)(2,1)S(1)}, u32[]{:S(2)}, u32[]{:S(2)}) %all-to-all-start) | async-done | bytes 524320 | tf_op jit(solution)/shard_map/all_to_all | solution.py:12
  29.2 1.7 %fusion.6 = f32[256,512]{1,0:T(8,128)S(1)} fusion(bf16[256,1024]{1,0:T(8,128)(2,1)S(1)} %bitcast.23, bf16[512,1024]{1,0:T(8,128)(2,1)} %param.6), kind=kOutput, calls=%fused_computation.18 | convolution fusion | flops 268435456 | bytes 2097152 | tf_op jit(solution)/shard_map/dot_general | solution.py:28
  30.9 0.0 collective-permute-done
  30.9 1.7 %fusion.7 = f32[256,512]{1,0:T(8,128)S(1)} fusion(bf16[256,1024]{1,0:T(8,128)(2,1)S(1)} %bitcast.24, bf16[512,1024]{1,0:T(8,128)(2,1)} %collective-permute-done), kind=kOutput, calls=%fused_computation.19 | convolution fusion | flops 268435456 | bytes 2097152 | tf_op jit(solution)/shard_map/dot_general | solution.py:28
  32.6 0.1 pad_maximum_fusion
  32.7 0.0 copy-start.1
  32.7 33.9 %all_to_all.30 = f32[16,16,1024]{2,1,0:T(8,128)} all-to-all(f32[16,16,1024]{2,1,0:T(8,128)S(1)} %bitcast.25), channel_id=1, replica_groups=mesh['y'=8,'xh'=2,'core'=2,'xl'=2,'z'=8] {'xl','z'}, dimensions={0} | all-to-all | bytes 2097152 | tf_op jit(solution)/shard_map/all_to_all | solution.py:12
  66.6 1.3 reduce_sum.27
  67.9 0.9 broadcast_in_dim.11
  68.8 6.7 %all-to-all-start.2 = ((bf16[16,16,1024]{2,1,0:T(8,128)(2,1)}), bf16[16,16,1024]{2,1,0:T(8,128)(2,1)}, u32[]{:S(2)}, u32[]{:S(2)}) async-start(bf16[16,16,1024]{2,1,0:T(8,128)(2,1)} %broadcast_in_dim.11), calls=%async_computation.2 | async-start | bytes 1048576 | tf_op jit(solution)/shard_map/all_to_all | solution.py:12
  75.5 0.0 copy-done.1
  75.5 4.0 %collective-permute-start.1 = (bf16[512,1024]{1,0:T(8,128)(2,1)S(1)}, bf16[512,1024]{1,0:T(8,128)(2,1)}, u32[]{:S(2)}, u32[]{:S(2)}) collective-permute-start(bf16[512,1024]{1,0:T(8,128)(2,1)S(1)} %copy-done.1), channel_id=1, source_target_pairs={{0,16},{16,0},{1,17},{17,1},{2,18},{18,2},{3,19},{19,3},{4,20},{20... | collective-permute-start | bytes 3145736 | tf_op jit(solution)/shard_map/ppermute | solution.py:41
  79.5 8.9 %all-to-all-done.2 = bf16[16,16,1024]{2,1,0:T(8,128)(2,1)} async-done(((bf16[16,16,1024]{2,1,0:T(8,128)(2,1)}), bf16[16,16,1024]{2,1,0:T(8,128)(2,1)}, u32[]{:S(2)}, u32[]{:S(2)}) %all-to-all-start.2) | async-done | bytes 524320 | tf_op jit(solution)/shard_map/all_to_all | solution.py:12
  88.4 1.4 fusion.4
  89.8 0.0 collective-permute-done.1
  89.8 2.6 %fusion = bf16[256,1024]{1,0:T(8,128)(2,1)} fusion(f32[256,1024]{1,0:T(8,128)S(1)} %fusion.4, bf16[512,1024]{1,0:T(8,128)(2,1)} %collective-permute-done.1, bf16[256,1024]{1,0:T(8,128)(2,1)} %bitcast.3), kind=kOutput, calls=%fused_computation.1 | convolution fusion | flops 268959744 | bytes 2883584 | tf_op jit(solution)/shard_map/dot_general | solution.py:32
  92.4 0.0 copy-start.2
  92.4 6.7 %all-to-all-start.3 = ((bf16[16,16,1024]{2,1,0:T(8,128)(2,1)}), bf16[16,16,1024]{2,1,0:T(8,128)(2,1)}, u32[]{:S(2)}, u32[]{:S(2)}) async-start(bf16[16,16,1024]{2,1,0:T(8,128)(2,1)} %bitcast.26), calls=%async_computation.3 | async-start | bytes 1048576 | tf_op jit(solution)/shard_map/all_to_all | solution.py:12
  99.1 0.0 copy-done
  99.1 1.0 constant_dynamic-slice_fusion
  100.1 1.2 copy.9
  101.3 0.8 dynamic_slice.7
  102.1 11.6 %all-to-all-done.3 = bf16[16,16,1024]{2,1,0:T(8,128)(2,1)} async-done(((bf16[16,16,1024]{2,1,0:T(8,128)(2,1)}), bf16[16,16,1024]{2,1,0:T(8,128)(2,1)}, u32[]{:S(2)}, u32[]{:S(2)}) %all-to-all-start.3) | async-done | bytes 524320 | tf_op jit(solution)/shard_map/all_to_all | solution.py:12
  113.7 1.1 convert_reduce_fusion.1
  114.8 0.0 copy-done.2
  114.9 0.1 multiply_convert_fusion
  114.9 0.1 broadcast_in_dim.13
  115.0 19.1 %all_to_all.31 = bf16[16,16,1024]{2,1,0:T(8,128)(2,1)S(1)} all-to-all(bf16[16,16,1024]{2,1,0:T(8,128)(2,1)S(1)} %broadcast_in_dim.13), channel_id=1, replica_groups=mesh['y'=8,'xh'=2,'core'=2,'xl'=2,'z'=8] {'y','xh'}, dimensions={0} | all-to-all | bytes 1048576 | tf_op jit(solution)/shard_map/all_to_all | solution.py:12
  134.1 1.7 %convolution_convert_fusion = bf16[16,16,512]{2,1,0:T(8,128)(2,1)S(1)} fusion(bf16[16,16,1024]{2,1,0:T(8,128)(2,1)S(1)} %all_to_all.31, bf16[512,1024]{1,0:T(8,128)(2,1)} %collective-permute-done.1), kind=kOutput, calls=%fused_computation.2 | convolution fusion | flops 268566528 | bytes 1835008 | tf_op jit(solution)/shard_map/dot_general | solution.py:28
  135.8 0.5 convolution_convert_fusion.1
  136.3 0.1 pad_maximum_fusion.1
  136.3 23.6 %all_to_all.32 = bf16[16,16,1024]{2,1,0:T(8,128)(2,1)S(1)} all-to-all(bf16[16,16,1024]{2,1,0:T(8,128)(2,1)S(1)} %pad_maximum_fusion.1), channel_id=1, replica_groups=mesh['y'=8,'xh'=2,'core'=2,'xl'=2,'z'=8] {'xl','z'}, dimensions={0} | all-to-all | bytes 1048576 | tf_op jit(solution)/shard_map/all_to_all | solution.py:12
  159.9 0.1 convert_reduce_fusion
  160.0 5.5 %collective-permute-start.2 = (f32[16,512]{1,0:T(8,128)S(1)}, f32[16,512]{1,0:T(8,128)S(1)}, u32[]{:S(2)}, u32[]{:S(2)}) collective-permute-start(f32[16,512]{1,0:T(8,128)S(1)} %slice.19), channel_id=1, source_target_pairs={{0,16},{16,0},{1,17},{17,1},{2,18},{18,2},{3,19},{19,3},{4,20},{20... | collective-permute-start | bytes 98312 | tf_op jit(solution)/shard_map/ppermute | solution.py:56
  165.5 0.8 collective-permute-done.2
  166.4 0.6 maximum_bitcast_fusion
  (2 shorter events, 0.0 us)
Async XLA Ops:
  0.0 99.1 %copy-start = (s32[1024,512]{1,0:T(8,128)S(1)}, s32[1024,512]{1,0:T(8,128)}, u32[]{:S(2)}) copy-start(s32[1024,512]{1,0:T(8,128)} %param.9) | copy-start | bytes 6291460
  1.8 27.4 %all-to-all-start = ((bf16[16,16,1024]{2,1,0:T(8,128)(2,1)}), bf16[16,16,1024]{2,1,0:T(8,128)(2,1)S(1)}, u32[]{:S(2)}, u32[]{:S(2)}) async-start(bf16[16,16,1024]{2,1,0:T(8,128)(2,1)} %broadcast_in_dim.10), calls=%async_computation | async-start | bytes 1048576 | tf_op jit(solution)/shard_map/all_to_all | solution.py:12
  12.0 18.9 %collective-permute-start = (bf16[512,1024]{1,0:T(8,128)(2,1)}, bf16[512,1024]{1,0:T(8,128)(2,1)}, u32[]{:S(2)}, u32[]{:S(2)}) collective-permute-start(bf16[512,1024]{1,0:T(8,128)(2,1)} %param.6), channel_id=1, source_target_pairs={{0,16},{16,0},{1,17},{17,1},{2,18},{18,2},{3,19},{19,3},{4,20},{20... | collective-permute-start | bytes 3145736 | tf_op jit(solution)/shard_map/ppermute | solution.py:40
  32.7 42.7 %copy-start.1 = (bf16[512,1024]{1,0:T(8,128)(2,1)S(1)}, bf16[512,1024]{1,0:T(8,128)(2,1)}, u32[]{:S(2)}) copy-start(bf16[512,1024]{1,0:T(8,128)(2,1)} %param.7) | copy-start | bytes 3145732
  68.8 19.7 %all-to-all-start.2 = ((bf16[16,16,1024]{2,1,0:T(8,128)(2,1)}), bf16[16,16,1024]{2,1,0:T(8,128)(2,1)}, u32[]{:S(2)}, u32[]{:S(2)}) async-start(bf16[16,16,1024]{2,1,0:T(8,128)(2,1)} %broadcast_in_dim.11), calls=%async_computation.2 | async-start | bytes 1048576 | tf_op jit(solution)/shard_map/all_to_all | solution.py:12
  75.5 14.4 %collective-permute-start.1 = (bf16[512,1024]{1,0:T(8,128)(2,1)S(1)}, bf16[512,1024]{1,0:T(8,128)(2,1)}, u32[]{:S(2)}, u32[]{:S(2)}) collective-permute-start(bf16[512,1024]{1,0:T(8,128)(2,1)S(1)} %copy-done.1), channel_id=1, source_target_pairs={{0,16},{16,0},{1,17},{17,1},{2,18},{18,2},{3,19},{19,3},{4,20},{20... | collective-permute-start | bytes 3145736 | tf_op jit(solution)/shard_map/ppermute | solution.py:41
  92.4 22.5 %copy-start.2 = (f32[1024]{0:T(1024)S(1)}, f32[1024]{0:T(1024)}, u32[]{:S(2)}) copy-start(f32[1024]{0:T(1024)} %param.10) | copy-start | bytes 12292
  92.4 21.3 %all-to-all-start.3 = ((bf16[16,16,1024]{2,1,0:T(8,128)(2,1)}), bf16[16,16,1024]{2,1,0:T(8,128)(2,1)}, u32[]{:S(2)}, u32[]{:S(2)}) async-start(bf16[16,16,1024]{2,1,0:T(8,128)(2,1)} %bitcast.26), calls=%async_computation.3 | async-start | bytes 1048576 | tf_op jit(solution)/shard_map/all_to_all | solution.py:12
  160.0 6.4 %collective-permute-start.2 = (f32[16,512]{1,0:T(8,128)S(1)}, f32[16,512]{1,0:T(8,128)S(1)}, u32[]{:S(2)}, u32[]{:S(2)}) collective-permute-start(f32[16,512]{1,0:T(8,128)S(1)} %slice.19), channel_id=1, source_target_pairs={{0,16},{16,0},{1,17},{17,1},{2,18},{18,2},{3,19},{19,3},{4,20},{20... | collective-permute-start | bytes 98312 | tf_op jit(solution)/shard_map/ppermute | solution.py:56

commit v2 on v1

v2 whole, which is shorter than its diff:
```python
import jax
import jax.numpy as jnp
from jax import lax
from jax.experimental import pallas as pl
from jax.experimental.pallas import tpu as pltpu
from jax.sharding import Mesh, PartitionSpec as P


ROW = ("y", "xh")
COL = ("xl", "z")
BF16, F32 = jnp.bfloat16, jnp.float32
NT = (((1,), (1,)), ((), ()))
NN = (((1,), (0,)), ((), ()))


def exchange(pieces, axes):
    return lax.all_to_all(pieces, axes, 0, 0)


def local(kernel, out, *operands):
    one = not isinstance(out, list)
    outs = [jax.ShapeDtypeStruct(*o) for o in ([out] if one else out)]
    vmem = pl.BlockSpec(memory_space=pltpu.VMEM)
    got = pl.pallas_call(
        kernel,
        out_shape=outs,
        in_specs=[vmem if o.ndim > 1 else pl.BlockSpec(memory_space=pltpu.SMEM) for o in operands],
        out_specs=[vmem for _ in outs],
        compiler_params=pltpu.CompilerParams(vmem_limit_bytes=24 * 2**20),
        cost_estimate=pl.CostEstimate(
            flops=2048 * operands[0].size,
            transcendentals=0,
            bytes_accessed=sum(o.nbytes for o in operands),
        ),
    )(*operands)
    return got[0] if one else got


def total(ref):
    acc = ref[0].astype(F32)
    for k in range(1, ref.shape[0]):
        acc += ref[k].astype(F32)
    return acc


def stream_kernel(left_hbm, own_hbm, other_hbm, out_ref, left_ref, pert_ref, sem):
    rows, cols = own_hbm.shape
    cut = rows // 2
    copies = [pltpu.make_async_copy(left_hbm, left_ref, sem.at[4])]
    for k in range(4):
        src = (own_hbm, other_hbm)[k // 2].at[pl.ds(k % 2 * cut, cut)]
        copies.append(pltpu.make_async_copy(src, pert_ref.at[k], sem.at[k]))
    for copy in copies:
        copy.start()
    copies[0].wait()
    left = left_ref[...].reshape(-1, cols)
    for k in range(4):
        copies[1 + k].wait()
        part = lax.dot_general(left, pert_ref[k], NT, preferred_element_type=F32)
        out_ref[:, :, k * cut : (k + 1) * cut] = part.astype(BF16).reshape(
            out_ref.shape[0], out_ref.shape[1], cut
        )


def image_kernel(left_ref, own_ref, other_ref, out_ref):
    left = left_ref[...].reshape(-1, left_ref.shape[-1])
    rows = own_ref.shape[0]
    for k, ref in enumerate((own_ref, other_ref)):
        part = lax.dot_general(left, ref[...], NT, preferred_element_type=F32)
        out_ref[:, :, k * rows : (k + 1) * rows] = part.astype(BF16).reshape(
            out_ref.shape[0], out_ref.shape[1], rows
        )


def projection_kernel(left_ref, own_ref, other_ref, out_ref):
    rows = own_ref.shape[0]
    left = left_ref[...].reshape(-1, left_ref.shape[-1])
    part = lax.dot_general(left[:, :rows], own_ref[...], NN, preferred_element_type=F32)
    part += lax.dot_general(left[:, rows:], other_ref[...], NN, preferred_element_type=F32)
    out_ref[...] = part.astype(BF16).reshape(out_ref.shape)


def sum_kernel(got_ref, out_ref):
    out_ref[...] = jnp.broadcast_to(total(got_ref).astype(BF16)[None], out_ref.shape)


def scale_kernel(got_ref, weight_ref, out_ref):
    coef = (total(got_ref) * weight_ref[...]).astype(BF16)
    out_ref[...] = jnp.broadcast_to(coef[None], out_ref.shape)


def final_kernel(got_ref, own_ref, other_ref):
    rows = own_ref.shape[1]
    acc = total(got_ref)
    own_ref[...] = acc[:, :rows]
    other_ref[...] = acc[:, rows:]


def place_kernel(core_ref, own_ref, got_ref, out_ref):
    width = own_ref.shape[0]
    flip = core_ref[0] == 1
    own, got = own_ref[...], got_ref[...]
    out_ref[:width] = jnp.where(flip, got, own)
    out_ref[width:] = jnp.where(flip, own, got)


def steps(perturbation, basis, orbitals, pair_mask, energies, occ_energies):
    swap = [(0, 1), (1, 0)]
    core = lax.axis_index("core")
    rows, cols = perturbation.shape
    width = orbitals.shape[1]
    n_row, n_col = lax.axis_size(ROW), lax.axis_size(COL)
    share = width * n_row // n_col
    pert_other = lax.ppermute(perturbation, "core", swap)
    basis_other = lax.ppermute(basis, "core", swap)
    first = lax.axis_index(ROW + ("core",)) * width
    mask_t = lax.dynamic_slice_in_dim(pair_mask, first, width, 1).T
    occ = lax.dynamic_slice_in_dim(occ_energies, first, width, 0)
    weight = jnp.where(mask_t == 1, 1.0 / (energies[None, :] - occ[:, None]), 0.0)

    orbs = exchange(jnp.broadcast_to(orbitals.T[None], (n_row, width, cols)), ROW)
    orbs, pert_other, basis_other, weight = lax.optimization_barrier(
        (orbs, pert_other, basis_other, weight)
    )
    by_col, by_row = ((n_col, share, 2 * rows), BF16), ((n_row, width, cols), BF16)
    hbm = pl.BlockSpec(memory_space=pltpu.MemorySpace.HBM)
    part = pl.pallas_call(
        stream_kernel,
        out_shape=jax.ShapeDtypeStruct(*by_col),
        in_specs=[hbm] * 3,
        out_specs=pl.BlockSpec(memory_space=pltpu.VMEM),
        scratch_shapes=[
            pltpu.VMEM(orbs.shape, BF16),
            pltpu.VMEM((4, rows // 2, cols), BF16),
            pltpu.SemaphoreType.DMA((5,)),
        ],
        compiler_params=pltpu.CompilerParams(vmem_limit_bytes=24 * 2**20),
        cost_estimate=pl.CostEstimate(
            flops=4 * orbs.size * rows, transcendentals=0, bytes_accessed=3 * orbs.nbytes
        ),
        name="image",
    )(orbs, perturbation, pert_other)
    part = exchange(part, COL)
    image = exchange(local(sum_kernel, by_col, part), COL)
    part = exchange(local(projection_kernel, by_row, image, basis, basis_other), ROW)
    coef = exchange(local(scale_kernel, by_row, part, weight), ROW)
    part = exchange(local(image_kernel, by_col, coef, basis, basis_other), COL)
    own, other = local(final_kernel, [((share, rows), F32)] * 2, part)
    got = lax.ppermute(other, "core", swap)
    return local(place_kernel, ((2 * share, rows), F32), core.reshape(1), own, got).T


def solution(mesh):
    sizes = (mesh.shape["row"] // 4, 2, 2, 2, mesh.shape["col"] // 2)
    fine = Mesh(mesh.devices.reshape(sizes), ("y", "xh", "core", "xl", "z"))
    row, col = ("y", "xh", "core"), ("xl", "z")
    return jax.shard_map(
        steps,
        mesh=fine,
        in_specs=(P(row, col), P(row, col), P(col, row), P(col, None), P(col), P()),
        out_specs=P(row, col),
        check_vma=False,
    )
```

time: 168 us -> 153 us (0.911)
  blocking collectives: 76.5 us -> 105 us
  waiting for transfers between devices: 35.7 us -> 15.1 us
  starting transfers between devices: 36 us -> 20.6 us
  matrix products: 9.52 us -> 0 us
  Pallas kernels: 0 us -> 5.26 us
  other arithmetic: 3.36 us -> 0.09 us
    all_to_all x3 -> x5, blocking collectives: 76.5 us -> 105 us  [exchange(): return lax.all_to_all(pieces, axes, 0, 0)]
    all_to_all x3 -> x1, waiting for transfers between devices: 34.9 us -> 14.3 us  [exchange(): return lax.all_to_all(pieces, axes, 0, 0)]
    all_to_all x3 -> x1, starting transfers between devices: 23.6 us -> 4.24 us  [exchange(): return lax.all_to_all(pieces, axes, 0, 0)]
    dot_general x6 -> x0, matrix products: 9.52 us -> none  [the longest x4 5.57 us: dot_nt(): lax.dot_general(a, b, (((1,), (1,)), ((), ())), preferred_element_type=F32)]
    pallas_call x0 -> x7, Pallas kernels: none -> 5.26 us  [the longest x1 2.93 us: steps(): pl.pallas_call(stream_kernel, out_shape=jax.ShapeDtypeStruct(*by_col), in...]
    ppermute x3, starting transfers between devices: 12.4 us -> 16.3 us  [the longest x1 8.87 us: steps(): pert_other = lax.ppermute(perturbation, 'core', swap)]
    reduce_sum x3 -> x0, other arithmetic: 2.49 us -> none  [collect(): return exchange(pieces, axes).astype(F32).sum(axis=0)]
  transfers between devices with their start and end apart: 6 -> 4, of which waited for: 4 -> 2; matrix products, arithmetic and copies ran while one was open for 4% -> 3% of each run, Pallas kernels for 0% -> 0%
where the time goes in v2:
time: 153 us; the launch traced here: 152 us
  blocking collectives  105 us (69%)
  starting transfers between devices  20.6 us (13%)
  waiting for transfers between devices  15.1 us (10%)
  local copies, waits for them, and re-layouts  5.81 us (4%)
  Pallas kernels  5.26 us (3%)
    all_to_all x5, blocking collectives, exchange(): return lax.all_to_all(pieces, axes, 0, 0)  105 us
    all_to_all x1, waiting for transfers between devices, exchange(): return lax.all_to_all(pieces, axes, 0, 0)  14.3 us
    ppermute x1, starting transfers between devices, steps(): pert_other = lax.ppermute(perturbation, 'core', swap)  8.87 us
    ppermute x1, starting transfers between devices, steps(): got = lax.ppermute(other, 'core', swap)  5.53 us
    all_to_all x1, starting transfers between devices, exchange(): return lax.all_to_all(pieces, axes, 0, 0)  4.24 us
  transfers between devices with their start and end apart: 4, of which 2 were waited for; matrix products, arithmetic and copies ran while one was open for 3% of the time, Pallas kernels for 0%

profile of v2, /device:TPU:1, one launch (start us, length us, event | category | flops | bytes accessed | tf_op | source)
XLA Modules:
  0.0 152.1 jit_solution(10176039066557788475)
XLA Ops:
  0.0 0.0 copy-start
  0.0 0.0 copy-start.3
  0.0 8.9 %collective-permute-start = (bf16[512,1024]{1,0:T(8,128)(2,1)}, bf16[512,1024]{1,0:T(8,128)(2,1)}, u32[]{:S(2)}, u32[]{:S(2)}) collective-permute-start(bf16[512,1024]{1,0:T(8,128)(2,1)} %own_hbm.1), channel_id=1, source_target_pairs={{0,16},{16,0},{1,17},{17,1},{2,18},{18,2},{3,19},{19,3},{4,20},{20... | collective-permute-start | bytes 3145736 | tf_op jit(solution)/shard_map/ppermute | solution.py:114
  8.9 1.9 %collective-permute-start.1 = (bf16[512,1024]{1,0:T(8,128)(2,1)}, bf16[512,1024]{1,0:T(8,128)(2,1)S(1)}, u32[]{:S(2)}, u32[]{:S(2)}) collective-permute-start(bf16[512,1024]{1,0:T(8,128)(2,1)} %own_ref.3), channel_id=1, source_target_pairs={{0,16},{16,0},{1,17},{17,1},{2,18},{18,2},{3,19},{19,3},{4,20},{20... | collective-permute-start | bytes 3145736 | tf_op jit(solution)/shard_map/ppermute | solution.py:115
  10.8 1.6 %broadcast_in_dim.6 = bf16[16,16,1024]{2,1,0:T(8,128)(2,1)} broadcast(bf16[16,1024]{1,0:T(8,128)(2,1)} %bitcast.5), dimensions={1,2} | broadcast | bytes 557056 | tf_op jit(solution)/shard_map/broadcast_in_dim | solution.py:121
  12.4 4.2 %all-to-all-start = ((bf16[16,16,1024]{2,1,0:T(8,128)(2,1)}), bf16[16,16,1024]{2,1,0:T(8,128)(2,1)}, u32[]{:S(2)}, u32[]{:S(2)}) async-start(bf16[16,16,1024]{2,1,0:T(8,128)(2,1)} %broadcast_in_dim.6), calls=%async_computation | async-start | bytes 1048576 | tf_op jit(solution)/shard_map/all_to_all | solution.py:17
  16.7 0.8 dynamic_slice.7
  17.4 0.0 copy-done
  17.4 1.0 constant_dynamic-slice_fusion
  18.5 1.2 copy.8
  19.7 0.0 copy-done.3
  19.7 0.1 divide_select_fusion.weight_ref
  19.8 14.3 %all-to-all-done.left_hbm = bf16[16,16,1024]{2,1,0:T(8,128)(2,1)} async-done(((bf16[16,16,1024]{2,1,0:T(8,128)(2,1)}), bf16[16,16,1024]{2,1,0:T(8,128)(2,1)}, u32[]{:S(2)}, u32[]{:S(2)}) %all-to-all-start) | async-done | bytes 524320 | tf_op jit(solution)/shard_map/all_to_all | solution.py:17
  34.0 0.0 collective-permute-done.other_hbm
  34.0 0.0 collective-permute-done.1.other_ref
  34.0 0.0 copy-start.2
  34.0 1.2 copy-done.2
  35.3 2.9 %image.1 = bf16[16,16,1024]{2,1,0:T(8,128)(2,1)S(1)} custom-call(bf16[16,16,1024]{2,1,0:T(8,128)(2,1)} %all-to-all-done.left_hbm, bf16[512,1024]{1,0:T(8,128)(2,1)S(1)} %copy-done.2, bf16[512,1024]{1,0:T(8,128)(2,1)} %collective-permute-done.other_hbm), custom_call_target="tpu_custom_call" | custom-call | flops 536870912 | bytes 1572864 | tf_op jit(solution)/shard_map/image/pallas_call | solution.py:127
  38.2 0.0 copy-start.1
  38.2 22.5 %all_to_all.30.got_ref = bf16[16,16,1024]{2,1,0:T(8,128)(2,1)S(1)} all-to-all(bf16[16,16,1024]{2,1,0:T(8,128)(2,1)S(1)} %image.1), channel_id=1, replica_groups=mesh['y'=8,'xh'=2,'core'=2,'xl'=2,'z'=8] {'xl','z'}, dimensions={0} | all-to-all | bytes 1048576 | tf_op jit(solution)/shard_map/all_to_all | solution.py:17
  60.7 0.1 shard_map.64
  60.8 18.9 %all_to_all.31.left_ref = bf16[16,16,1024]{2,1,0:T(8,128)(2,1)S(1)} all-to-all(bf16[16,16,1024]{2,1,0:T(8,128)(2,1)S(1)} %shard_map.64), channel_id=1, replica_groups=mesh['y'=8,'xh'=2,'core'=2,'xl'=2,'z'=8] {'xl','z'}, dimensions={0} | all-to-all | bytes 1048576 | tf_op jit(solution)/shard_map/all_to_all | solution.py:17
  79.7 0.0 copy-done.1
  79.7 0.7 shard_map.65
  80.4 22.0 %all_to_all.32.got_ref = bf16[16,16,1024]{2,1,0:T(8,128)(2,1)S(1)} all-to-all(bf16[16,16,1024]{2,1,0:T(8,128)(2,1)S(1)} %shard_map.65), channel_id=1, replica_groups=mesh['y'=8,'xh'=2,'core'=2,'xl'=2,'z'=8] {'y','xh'}, dimensions={0} | all-to-all | bytes 1048576 | tf_op jit(solution)/shard_map/all_to_all | solution.py:17
  102.4 0.1 shard_map.66
  102.5 18.8 %all_to_all.33.left_ref = bf16[16,16,1024]{2,1,0:T(8,128)(2,1)S(1)} all-to-all(bf16[16,16,1024]{2,1,0:T(8,128)(2,1)S(1)} %shard_map.66), channel_id=1, replica_groups=mesh['y'=8,'xh'=2,'core'=2,'xl'=2,'z'=8] {'y','xh'}, dimensions={0} | all-to-all | bytes 1048576 | tf_op jit(solution)/shard_map/all_to_all | solution.py:17
  121.3 0.7 shard_map.67
  122.1 22.9 %all_to_all.34.got_ref = bf16[16,16,1024]{2,1,0:T(8,128)(2,1)S(1)} all-to-all(bf16[16,16,1024]{2,1,0:T(8,128)(2,1)S(1)} %shard_map.67), channel_id=1, replica_groups=mesh['y'=8,'xh'=2,'core'=2,'xl'=2,'z'=8] {'xl','z'}, dimensions={0} | all-to-all | bytes 1048576 | tf_op jit(solution)/shard_map/all_to_all | solution.py:17
  145.0 0.1 shard_map.68
  145.1 5.5 %collective-permute-start.2 = (f32[16,512]{1,0:T(8,128)S(1)}, f32[16,512]{1,0:T(8,128)S(1)}, u32[]{:S(2)}, u32[]{:S(2)}) collective-permute-start(f32[16,512]{1,0:T(8,128)S(1)} %get-tuple-element.16), channel_id=1, source_target_pairs={{0,16},{16,0},{1,17},{17,1},{2,18},{18,2},{3,19},{19,3},{4,20},{20... | collective-permute-start | bytes 98312 | tf_op jit(solution)/shard_map/ppermute | solution.py:149
  150.6 0.8 collective-permute-done.2.got_ref
  151.5 0.6 shard_map.69
Async XLA Ops:
  0.0 17.4 %copy-start = (s32[1024,512]{1,0:T(8,128)S(1)}, s32[1024,512]{1,0:T(8,128)}, u32[]{:S(2)}) copy-start(s32[1024,512]{1,0:T(8,128)} %param.9) | copy-start | bytes 6291460
  0.0 19.7 %copy-start.3 = (f32[1024]{0:T(1024)S(1)}, f32[1024]{0:T(1024)}, u32[]{:S(2)}) copy-start(f32[1024]{0:T(1024)} %param.10) | copy-start | bytes 12292
  0.0 34.0 %collective-permute-start = (bf16[512,1024]{1,0:T(8,128)(2,1)}, bf16[512,1024]{1,0:T(8,128)(2,1)}, u32[]{:S(2)}, u32[]{:S(2)}) collective-permute-start(bf16[512,1024]{1,0:T(8,128)(2,1)} %own_hbm.1), channel_id=1, source_target_pairs={{0,16},{16,0},{1,17},{17,1},{2,18},{18,2},{3,19},{19,3},{4,20},{20... | collective-permute-start | bytes 3145736 | tf_op jit(solution)/shard_map/ppermute | solution.py:114
  8.9 25.2 %collective-permute-start.1 = (bf16[512,1024]{1,0:T(8,128)(2,1)}, bf16[512,1024]{1,0:T(8,128)(2,1)S(1)}, u32[]{:S(2)}, u32[]{:S(2)}) collective-permute-start(bf16[512,1024]{1,0:T(8,128)(2,1)} %own_ref.3), channel_id=1, source_target_pairs={{0,16},{16,0},{1,17},{17,1},{2,18},{18,2},{3,19},{19,3},{4,20},{20... | collective-permute-start | bytes 3145736 | tf_op jit(solution)/shard_map/ppermute | solution.py:115
  12.4 21.6 %all-to-all-start = ((bf16[16,16,1024]{2,1,0:T(8,128)(2,1)}), bf16[16,16,1024]{2,1,0:T(8,128)(2,1)}, u32[]{:S(2)}, u32[]{:S(2)}) async-start(bf16[16,16,1024]{2,1,0:T(8,128)(2,1)} %broadcast_in_dim.6), calls=%async_computation | async-start | bytes 1048576 | tf_op jit(solution)/shard_map/all_to_all | solution.py:17
  34.0 1.2 copy-start.2
  38.2 41.5 %copy-start.1 = (bf16[512,1024]{1,0:T(8,128)(2,1)S(1)}, bf16[512,1024]{1,0:T(8,128)(2,1)}, u32[]{:S(2)}) copy-start(bf16[512,1024]{1,0:T(8,128)(2,1)} %own_ref.3) | copy-start | bytes 3145732
  145.1 6.4 %collective-permute-start.2 = (f32[16,512]{1,0:T(8,128)S(1)}, f32[16,512]{1,0:T(8,128)S(1)}, u32[]{:S(2)}, u32[]{:S(2)}) collective-permute-start(f32[16,512]{1,0:T(8,128)S(1)} %get-tuple-element.16), channel_id=1, source_target_pairs={{0,16},{16,0},{1,17},{17,1},{2,18},{18,2},{3,19},{19,3},{4,20},{20... | collective-permute-start | bytes 98312 | tf_op jit(solution)/shard_map/ppermute | solution.py:149

commit v3 on v1

v3 whole, which is shorter than its diff:
```python
import jax
import jax.numpy as jnp
from jax import lax
from jax.experimental import pallas as pl
from jax.experimental.pallas import tpu as pltpu
from jax.sharding import Mesh, PartitionSpec as P


ROW = ("y", "xh")
COL = ("xl", "z")
BF16, F32 = jnp.bfloat16, jnp.float32
NT = (((1,), (1,)), ((), ()))
NN = (((1,), (0,)), ((), ()))


def exchange(pieces, axes):
    return lax.all_to_all(pieces, axes, 0, 0)


def local(kernel, outs, *operands, scratch=(), hbm=()):
    places = [
        pltpu.SMEM if o.ndim == 1 else pl.ANY if k in hbm else pltpu.VMEM
        for k, o in enumerate(operands)
    ]
    return pl.pallas_call(
        kernel,
        out_shape=[jax.ShapeDtypeStruct(*o) for o in outs],
        in_specs=[pl.BlockSpec(memory_space=p) for p in places],
        out_specs=[pl.BlockSpec(memory_space=pltpu.VMEM) for _ in outs],
        scratch_shapes=list(scratch),
        compiler_params=pltpu.CompilerParams(vmem_limit_bytes=24 * 2**20),
        cost_estimate=pl.CostEstimate(
            flops=2**29, transcendentals=0, bytes_accessed=sum(o.nbytes for o in operands)
        ),
    )(*operands)


def put(part, lo, out_ref, acc_ref):
    cols = slice(lo, lo + part.shape[1])
    out_ref[:, :, cols] = part.astype(BF16).reshape(*out_ref.shape[:2], part.shape[1])
    acc_ref[:, cols] = part


def finish(at_ref, fix_ref, acc_ref):
    width = fix_ref.shape[0]
    kept = acc_ref[pl.ds(pl.multiple_of(at_ref[0] * width, width), width), :]
    fix_ref[...] = kept - kept.astype(BF16).astype(F32)


def total(got_ref, fix_ref):
    acc = fix_ref[...]
    for k in range(got_ref.shape[0]):
        acc += got_ref[k].astype(F32)
    return acc


def image_kernel(at_ref, left_ref, own_ref, other_hbm, out_ref, fix_ref, acc_ref, other_ref, sem):
    rows, cols = own_ref.shape
    cut = rows // 2
    copies = [
        pltpu.make_async_copy(other_hbm.at[pl.ds(k * cut, cut)], other_ref.at[k], sem.at[k])
        for k in range(2)
    ]
    for copy in copies:
        copy.start()
    left = left_ref[...].reshape(-1, cols)
    put(lax.dot_general(left, own_ref[...], NT, preferred_element_type=F32), 0, out_ref, acc_ref)
    for k in range(2):
        copies[k].wait()
        part = lax.dot_general(left, other_ref[k], NT, preferred_element_type=F32)
        put(part, rows + k * cut, out_ref, acc_ref)
    finish(at_ref, fix_ref, acc_ref)


def projection_kernel(at_ref, left_ref, own_ref, other_ref, out_ref, fix_ref, acc_ref):
    rows = own_ref.shape[0]
    left = left_ref[...].reshape(-1, left_ref.shape[-1])
    part = lax.dot_general(left[:, :rows], own_ref[...], NN, preferred_element_type=F32)
    part += lax.dot_general(left[:, rows:], other_ref[...], NN, preferred_element_type=F32)
    put(part, 0, out_ref, acc_ref)
    finish(at_ref, fix_ref, acc_ref)


def response_kernel(at_ref, left_ref, own_ref, other_ref, out_ref, fix_ref, acc_ref):
    rows, cols = own_ref.shape
    left = left_ref[...].reshape(-1, cols)
    for k, ref in enumerate((own_ref, other_ref)):
        part = lax.dot_general(left, ref[...], NT, preferred_element_type=F32)
        put(part, k * rows, out_ref, acc_ref)
    finish(at_ref, fix_ref, acc_ref)


def sum_kernel(got_ref, fix_ref, out_ref):
    image = total(got_ref, fix_ref).astype(BF16)
    out_ref[...] = jnp.broadcast_to(image[None], out_ref.shape)


def scale_kernel(got_ref, fix_ref, weight_ref, out_ref):
    coef = (total(got_ref, fix_ref) * weight_ref[...]).astype(BF16)
    out_ref[...] = jnp.broadcast_to(coef[None], out_ref.shape)


def final_kernel(got_ref, fix_ref, own_ref, other_ref):
    rows = own_ref.shape[1]
    acc = total(got_ref, fix_ref)
    own_ref[...] = acc[:, :rows]
    other_ref[...] = acc[:, rows:]


def place_kernel(core_ref, own_ref, got_ref, out_ref):
    width = own_ref.shape[0]
    flip = core_ref[0] == 1
    own, got = own_ref[...], got_ref[...]
    out_ref[:width] = jnp.where(flip, got, own)
    out_ref[width:] = jnp.where(flip, own, got)


def weights_kernel(at_ref, mask_hbm, energies_ref, occ_ref, out_ref, mask_ref, mask_t_ref, occ_t_ref, sem):
    lanes = occ_ref.shape[1]
    copy = pltpu.make_async_copy(
        mask_hbm.at[:, pl.ds(pl.multiple_of(at_ref[0] * lanes, lanes), lanes)], mask_ref, sem
    )
    copy.start()
    occ_t_ref[...] = jnp.broadcast_to(occ_ref[pl.ds(at_ref[0], 1), :], (lanes, lanes)).T
    copy.wait()
    mask_t_ref[...] = mask_ref[...].T
    rows = pl.ds(pl.multiple_of(at_ref[1], out_ref.shape[0]), out_ref.shape[0])
    spacing = energies_ref[...] - occ_t_ref[rows, :][:, :1]
    out_ref[...] = jnp.where(mask_t_ref[rows, :] == 1, 1.0 / spacing, 0.0)


def weights(mask, energies, occ, width):
    lanes, cols = 128, mask.shape[0]
    first = lax.axis_index(ROW + ("core",)) * width
    return local(
        weights_kernel,
        [((width, cols), F32)],
        jnp.stack([lax.div(first, lanes), lax.rem(first, lanes)]),
        mask,
        energies.reshape(1, cols),
        occ.reshape(-1, lanes),
        hbm=(1,),
        scratch=(
            pltpu.VMEM((cols, lanes), mask.dtype),
            pltpu.VMEM((lanes, cols), mask.dtype),
            pltpu.VMEM((lanes, lanes), F32),
            pltpu.SemaphoreType.DMA,
        ),
    )[0]


def steps(perturbation, basis, orbitals, pair_mask, energies, occ_energies):
    swap = [(0, 1), (1, 0)]
    core = lax.axis_index("core")
    rows, cols = perturbation.shape
    width = orbitals.shape[1]
    n_row, n_col = lax.axis_size(ROW), lax.axis_size(COL)
    share = width * n_row // n_col
    pert_other = lax.ppermute(perturbation, "core", swap)
    basis_other = lax.ppermute(basis, "core", swap)
    weight = weights(pair_mask, energies, occ_energies, width)
    orbs = exchange(jnp.broadcast_to(orbitals.T[None], (n_row, width, cols)), ROW)
    at_col, at_row = lax.axis_index(COL).reshape(1), lax.axis_index(ROW).reshape(1)
    orbs, pert_other, basis_other, weight, at_col, at_row, core = lax.optimization_barrier(
        (orbs, pert_other, basis_other, weight, at_col, at_row, core.reshape(1))
    )
    n_orb = width * n_row
    by_col = ((n_col, share, 2 * rows), BF16), ((share, 2 * rows), F32)
    by_row = ((n_row, width, cols), BF16), ((width, cols), F32)
    acc_col, acc_row = pltpu.VMEM((n_orb, 2 * rows), F32), pltpu.VMEM((n_orb, cols), F32)
    part, fix = local(
        image_kernel,
        by_col,
        at_col,
        orbs,
        perturbation,
        pert_other,
        hbm=(3,),
        scratch=(acc_col, pltpu.VMEM((2, rows // 2, cols), BF16), pltpu.SemaphoreType.DMA((2,))),
    )
    (image,) = local(sum_kernel, by_col[:1], exchange(part, COL), fix)
    image = exchange(image, COL)
    part, fix = local(
        projection_kernel, by_row, at_row, image, basis, basis_other, scratch=(acc_row,)
    )
    (coef,) = local(scale_kernel, by_row[:1], exchange(part, ROW), fix, weight)
    coef = exchange(coef, ROW)
    part, fix = local(response_kernel, by_col, at_col, coef, basis, basis_other, scratch=(acc_col,))
    own, other = local(final_kernel, [((share, rows), F32)] * 2, exchange(part, COL), fix)
    got = lax.ppermute(other, "core", swap)
    (out,) = local(place_kernel, [((2 * share, rows), F32)], core, own, got)
    return out.T


def solution(mesh):
    sizes = (mesh.shape["row"] // 4, 2, 2, 2, mesh.shape["col"] // 2)
    fine = Mesh(mesh.devices.reshape(sizes), ("y", "xh", "core", "xl", "z"))
    row, col = ("y", "xh", "core"), ("xl", "z")
    return jax.shard_map(
        steps,
        mesh=fine,
        in_specs=(P(row, col), P(row, col), P(col, row), P(col, None), P(col), P()),
        out_specs=P(row, col),
        check_vma=False,
    )
```

time: 168 us -> 151 us (0.90)
  blocking collectives: 76.5 us -> 105 us
  waiting for transfers between devices: 35.7 us -> 14.2 us
  starting transfers between devices: 36 us -> 20.3 us
  matrix products: 9.52 us -> 0 us
  Pallas kernels: 0 us -> 5.66 us
  other arithmetic: 3.36 us -> 0.08 us
    all_to_all x3 -> x5, blocking collectives: 76.5 us -> 105 us  [exchange(): return lax.all_to_all(pieces, axes, 0, 0)]
    all_to_all x3 -> x1, waiting for transfers between devices: 34.9 us -> 13.3 us  [exchange(): return lax.all_to_all(pieces, axes, 0, 0)]
    all_to_all x3 -> x1, starting transfers between devices: 23.6 us -> 4.04 us  [exchange(): return lax.all_to_all(pieces, axes, 0, 0)]
    dot_general x6 -> x0, matrix products: 9.52 us -> none  [the longest x4 5.57 us: dot_nt(): lax.dot_general(a, b, (((1,), (1,)), ((), ())), preferred_element_type=F32)]
    pallas_call x0 -> x8, Pallas kernels: none -> 5.66 us  [local(): pl.pallas_call(kernel, out_shape=[jax.ShapeDtypeStruct(*o) for o in outs]...]
    ppermute x3, starting transfers between devices: 12.4 us -> 16.3 us  [the longest x1 8.87 us: steps(): pert_other = lax.ppermute(perturbation, 'core', swap)]
    reduce_sum x3 -> x0, other arithmetic: 2.49 us -> none  [collect(): return exchange(pieces, axes).astype(F32).sum(axis=0)]
    dynamic_slice x2 -> x0, local copies, waits for them, and re-layouts: 1.77 us -> none  [the longest x1 1 us: shards(): mask_t = lax.dynamic_slice_in_dim(pair_mask, first, width, 1).T]
  transfers between devices with their start and end apart: 6 -> 4, of which waited for: 4 -> 2; matrix products, arithmetic and copies ran while one was open for 4% -> 1% of each run, Pallas kernels for 0% -> 1%
where the time goes in v3:
time: 151 us; the launch traced here: 150 us
  blocking collectives  105 us (70%)
  starting transfers between devices  20.3 us (13%)
  waiting for transfers between devices  14.2 us (9%)
  Pallas kernels  5.66 us (4%)
  local copies, waits for them, and re-layouts  4.62 us (3%)
    all_to_all x5, blocking collectives, exchange(): return lax.all_to_all(pieces, axes, 0, 0)  105 us
    all_to_all x1, waiting for transfers between devices, exchange(): return lax.all_to_all(pieces, axes, 0, 0)  13.3 us
    ppermute x1, starting transfers between devices, steps(): pert_other = lax.ppermute(perturbation, 'core', swap)  8.87 us
    pallas_call x8, Pallas kernels, local(): pl.pallas_call(kernel, out_shape=[jax.ShapeDtypeStruct(*o) for o in outs]...  5.66 us
    ppermute x1, starting transfers between devices, steps(): got = lax.ppermute(other, 'core', swap)  5.52 us
    all_to_all x1, starting transfers between devices, exchange(): return lax.all_to_all(pieces, axes, 0, 0)  4.04 us
  transfers between devices with their start and end apart: 4, of which 2 were waited for; matrix products, arithmetic and copies ran while one was open for 1% of the time, Pallas kernels for 1%

profile of v3, /device:TPU:1, one launch (start us, length us, event | category | flops | bytes accessed | tf_op | source)
XLA Modules:
  0.0 150.3 jit_solution(9326553130067558090)
XLA Ops:
  0.0 0.0 copy-start.2
  0.0 8.9 %collective-permute-start = (bf16[512,1024]{1,0:T(8,128)(2,1)}, bf16[512,1024]{1,0:T(8,128)(2,1)}, u32[]{:S(2)}, u32[]{:S(2)}) collective-permute-start(bf16[512,1024]{1,0:T(8,128)(2,1)} %own_ref.3), channel_id=1, source_target_pairs={{0,16},{16,0},{1,17},{17,1},{2,18},{18,2},{3,19},{19,3},{4,20},{20... | collective-permute-start | bytes 3145736 | tf_op jit(solution)/shard_map/ppermute | solution.py:159
  8.9 1.9 %collective-permute-start.1 = (bf16[512,1024]{1,0:T(8,128)(2,1)}, bf16[512,1024]{1,0:T(8,128)(2,1)S(1)}, u32[]{:S(2)}, u32[]{:S(2)}) collective-permute-start(bf16[512,1024]{1,0:T(8,128)(2,1)} %own_ref.5), channel_id=1, source_target_pairs={{0,16},{16,0},{1,17},{17,1},{2,18},{18,2},{3,19},{19,3},{4,20},{20... | collective-permute-start | bytes 3145736 | tf_op jit(solution)/shard_map/ppermute | solution.py:160
  10.8 1.6 %broadcast_in_dim.2 = bf16[16,16,1024]{2,1,0:T(8,128)(2,1)} broadcast(bf16[16,1024]{1,0:T(8,128)(2,1)} %bitcast.11), dimensions={1,2} | broadcast | bytes 557056 | tf_op jit(solution)/shard_map/broadcast_in_dim | solution.py:162
  12.5 4.0 %all-to-all-start = ((bf16[16,16,1024]{2,1,0:T(8,128)(2,1)}), bf16[16,16,1024]{2,1,0:T(8,128)(2,1)S(1)}, u32[]{:S(2)}, u32[]{:S(2)}) async-start(bf16[16,16,1024]{2,1,0:T(8,128)(2,1)} %broadcast_in_dim.2), calls=%async_computation | async-start | bytes 1048576 | tf_op jit(solution)/shard_map/all_to_all | solution.py:17
  16.5 0.1 pad_add_fusion.at_ref
  16.6 0.0 copy-start.1
  16.6 1.6 %copy-done.1 = s32[1024,512]{1,0:T(8,128)S(1)} copy-done((s32[1024,512]{1,0:T(8,128)S(1)}, s32[1024,512]{1,0:T(8,128)}, u32[]{:S(2)}) %copy-start.1) | copy-done | bytes 2097176
  18.2 0.0 copy-start.3
  18.2 0.7 copy-done.3
  18.9 0.0 copy-start.4
  18.9 0.7 copy-done.4
  19.6 1.0 shard_map.64.weight_ref
  20.5 13.3 %all-to-all-done.left_ref = bf16[16,16,1024]{2,1,0:T(8,128)(2,1)S(1)} async-done(((bf16[16,16,1024]{2,1,0:T(8,128)(2,1)}), bf16[16,16,1024]{2,1,0:T(8,128)(2,1)S(1)}, u32[]{:S(2)}, u32[]{:S(2)}) %all-to-all-start) | async-done | bytes 524320 | tf_op jit(solution)/shard_map/all_to_all | solution.py:17
  33.9 0.0 collective-permute-done.other_hbm
  33.9 0.0 collective-permute-done.1.other_ref
  33.9 0.0 copy-done.2
  33.9 2.3 %shard_map.65 = (bf16[16,16,1024]{2,1,0:T(8,128)(2,1)S(1)}, f32[16,1024]{1,0:T(8,128)S(1)}) custom-call(s32[1]{0:T(128)} %bitcast.5.at_ref, bf16[16,16,1024]{2,1,0:T(8,128)(2,1)S(1)} %all-to-all-done.left_ref, bf16[512,1024]{1,0:T(8,128)(2,1)S(1)} %copy-done.2, bf16[512,1024]{1,0:T(8,128)(2,1)} %collective-permute-done.other_hbm), custom_call_target="tpu_custom_call" | custom-call | flops 536870912 | bytes 2621444 | tf_op jit(solution)/shard_map/pallas_call | solution.py:25
  36.2 0.0 copy-start
  36.2 22.6 %all_to_all.30.got_ref = bf16[16,16,1024]{2,1,0:T(8,128)(2,1)S(1)} all-to-all(bf16[16,16,1024]{2,1,0:T(8,128)(2,1)S(1)} %get-tuple-element.25), channel_id=1, replica_groups=mesh['y'=8,'xh'=2,'core'=2,'xl'=2,'z'=8] {'xl','z'}, dimensions={0} | all-to-all | bytes 1048576 | tf_op jit(solution)/shard_map/all_to_all | solution.py:17
  58.8 0.1 shard_map.66
  58.9 18.9 %all_to_all.31.left_ref = bf16[16,16,1024]{2,1,0:T(8,128)(2,1)S(1)} all-to-all(bf16[16,16,1024]{2,1,0:T(8,128)(2,1)S(1)} %shard_map.66), channel_id=1, replica_groups=mesh['y'=8,'xh'=2,'core'=2,'xl'=2,'z'=8] {'xl','z'}, dimensions={0} | all-to-all | bytes 1048576 | tf_op jit(solution)/shard_map/all_to_all | solution.py:17
  77.8 0.0 copy-done
  77.8 0.7 shard_map.67
  78.5 22.0 %all_to_all.32.got_ref = bf16[16,16,1024]{2,1,0:T(8,128)(2,1)S(1)} all-to-all(bf16[16,16,1024]{2,1,0:T(8,128)(2,1)S(1)} %get-tuple-element.28), channel_id=1, replica_groups=mesh['y'=8,'xh'=2,'core'=2,'xl'=2,'z'=8] {'y','xh'}, dimensions={0} | all-to-all | bytes 1048576 | tf_op jit(solution)/shard_map/all_to_all | solution.py:17
  100.5 0.1 shard_map.68
  100.6 18.8 %all_to_all.33.left_ref = bf16[16,16,1024]{2,1,0:T(8,128)(2,1)S(1)} all-to-all(bf16[16,16,1024]{2,1,0:T(8,128)(2,1)S(1)} %shard_map.68), channel_id=1, replica_groups=mesh['y'=8,'xh'=2,'core'=2,'xl'=2,'z'=8] {'y','xh'}, dimensions={0} | all-to-all | bytes 1048576 | tf_op jit(solution)/shard_map/all_to_all | solution.py:17
  119.5 0.8 shard_map.69
  120.2 22.9 %all_to_all.34.got_ref = bf16[16,16,1024]{2,1,0:T(8,128)(2,1)S(1)} all-to-all(bf16[16,16,1024]{2,1,0:T(8,128)(2,1)S(1)} %get-tuple-element.31), channel_id=1, replica_groups=mesh['y'=8,'xh'=2,'core'=2,'xl'=2,'z'=8] {'xl','z'}, dimensions={0} | all-to-all | bytes 1048576 | tf_op jit(solution)/shard_map/all_to_all | solution.py:17
  143.2 0.1 shard_map.70
  143.3 5.5 %collective-permute-start.2 = (f32[16,512]{1,0:T(8,128)S(1)}, f32[16,512]{1,0:T(8,128)S(1)}, u32[]{:S(2)}, u32[]{:S(2)}) collective-permute-start(f32[16,512]{1,0:T(8,128)S(1)} %get-tuple-element.34), channel_id=1, source_target_pairs={{0,16},{16,0},{1,17},{17,1},{2,18},{18,2},{3,19},{19,3},{4,20},{20... | collective-permute-start | bytes 98312 | tf_op jit(solution)/shard_map/ppermute | solution.py:190
  148.8 0.8 collective-permute-done.2.got_ref
  149.6 0.6 shard_map.71
Async XLA Ops:
  0.0 33.9 %copy-start.2 = (bf16[512,1024]{1,0:T(8,128)(2,1)S(1)}, bf16[512,1024]{1,0:T(8,128)(2,1)}, u32[]{:S(2)}) copy-start(bf16[512,1024]{1,0:T(8,128)(2,1)} %own_ref.3) | copy-start | bytes 3145732
  0.0 33.9 %collective-permute-start = (bf16[512,1024]{1,0:T(8,128)(2,1)}, bf16[512,1024]{1,0:T(8,128)(2,1)}, u32[]{:S(2)}, u32[]{:S(2)}) collective-permute-start(bf16[512,1024]{1,0:T(8,128)(2,1)} %own_ref.3), channel_id=1, source_target_pairs={{0,16},{16,0},{1,17},{17,1},{2,18},{18,2},{3,19},{19,3},{4,20},{20... | collective-permute-start | bytes 3145736 | tf_op jit(solution)/shard_map/ppermute | solution.py:159
  8.9 25.0 %collective-permute-start.1 = (bf16[512,1024]{1,0:T(8,128)(2,1)}, bf16[512,1024]{1,0:T(8,128)(2,1)S(1)}, u32[]{:S(2)}, u32[]{:S(2)}) collective-permute-start(bf16[512,1024]{1,0:T(8,128)(2,1)} %own_ref.5), channel_id=1, source_target_pairs={{0,16},{16,0},{1,17},{17,1},{2,18},{18,2},{3,19},{19,3},{4,20},{20... | collective-permute-start | bytes 3145736 | tf_op jit(solution)/shard_map/ppermute | solution.py:160
  12.5 21.4 %all-to-all-start = ((bf16[16,16,1024]{2,1,0:T(8,128)(2,1)}), bf16[16,16,1024]{2,1,0:T(8,128)(2,1)S(1)}, u32[]{:S(2)}, u32[]{:S(2)}) async-start(bf16[16,16,1024]{2,1,0:T(8,128)(2,1)} %broadcast_in_dim.2), calls=%async_computation | async-start | bytes 1048576 | tf_op jit(solution)/shard_map/all_to_all | solution.py:17
  16.6 1.6 %copy-start.1 = (s32[1024,512]{1,0:T(8,128)S(1)}, s32[1024,512]{1,0:T(8,128)}, u32[]{:S(2)}) copy-start(s32[1024,512]{1,0:T(8,128)} %mask_hbm.1) | copy-start | bytes 6291460
  18.2 0.7 copy-start.3
  18.9 0.7 copy-start.4
  36.2 41.6 %copy-start = (bf16[512,1024]{1,0:T(8,128)(2,1)S(1)}, bf16[512,1024]{1,0:T(8,128)(2,1)}, u32[]{:S(2)}) copy-start(bf16[512,1024]{1,0:T(8,128)(2,1)} %own_ref.5) | copy-start | bytes 3145732
  143.3 6.4 %collective-permute-start.2 = (f32[16,512]{1,0:T(8,128)S(1)}, f32[16,512]{1,0:T(8,128)S(1)}, u32[]{:S(2)}, u32[]{:S(2)}) collective-permute-start(f32[16,512]{1,0:T(8,128)S(1)} %get-tuple-element.34), channel_id=1, source_target_pairs={{0,16},{16,0},{1,17},{17,1},{2,18},{18,2},{3,19},{19,3},{4,20},{20... | collective-permute-start | bytes 98312 | tf_op jit(solution)/shard_map/ppermute | solution.py:190
